TPU v7x, 256 devices: a whole 4x4x8 slice. The times are simulated.
256 devices in a mesh: seq: 64 (over y, z_hi, x, core), dp: 4 (over z_lo).
Axes of the slice: x: 4, y: 4, z: 8 (z_hi: 2, z_lo: 4; z = z_hi * 4 + z_lo), core: 2. Of those that a mesh axis runs over, the one named last changes fastest.
Arguments:
- inputs: bfloat16 [4, 64, 512, 512], P('dp', 'seq'), may hold values from -16 to 16
- norm_gain: float32 [512], replicated, may hold values from 0.25 to 1.75
- qkv_weight: bfloat16 [512, 1536], replicated, may hold values from -2 to 2
- out_weight: bfloat16 [512, 512], replicated, may hold values from -0.25 to 0.25
- out_cotan: bfloat16 [4, 64, 512, 512], P('dp', 'seq'), may hold values from -6 to 6
Outputs:
- input_grad: bfloat16 [4, 64, 512, 512], P('dp', 'seq')
- qkv_weight_grad: float32 [512, 1536], P('seq')
- out_weight_grad: float32 [512, 512], P('seq')
- gain_grad: float32 [512], P('seq')
All inputs are finite; a program needn't handle non-finite values.
Results may differ from a plain program's by a relative error of at most 0.0091.
Values may be sent and summed in bfloat16 or wider, within the bound.
A program may use at most 64 MiB of HBM per device.

v0:
```python
import math
import jax
import jax.numpy as jnp
from jax import lax
from jax.sharding import PartitionSpec as P

H = 8
HD = 64


def blocked(kernel, arrays, group_size):
    block_count = arrays[0].shape[0] // group_size
    split_arrays = tuple(
        (member.reshape((block_count, group_size) + member.shape[1:]) for member in arrays)
    )
    result = lax.map(lambda pieces: kernel(*pieces), split_arrays)
    return jax.tree.map(
        lambda member: member.reshape((block_count * group_size,) + member.shape[2:]), result
    )


def attend_probs(queries, key_vals):
    score_scale = HD ** (-0.5)
    scores = (
        jnp.einsum("glhd,gmhd->ghlm", queries, key_vals, preferred_element_type=jnp.float32)
        * score_scale
    )
    length = queries.shape[1]
    causal = lax.broadcasted_iota(jnp.int32, (length, length), 0) >= lax.broadcasted_iota(
        jnp.int32, (length, length), 1
    )
    scores = jnp.where(causal, scores, -1e30)
    row_max = jnp.max(scores, -1, keepdims=True)
    exponent = jnp.exp(scores - row_max)
    return exponent / jnp.sum(exponent, -1, keepdims=True)


def forward_block(queries, key_vals, values):
    weights = attend_probs(queries, key_vals).astype(jnp.bfloat16)
    return jnp.einsum(
        "ghlm,gmhd->glhd", weights, values, preferred_element_type=jnp.float32
    ).astype(jnp.bfloat16)


def backward_block(queries, key_vals, values, attended, cotangent):
    score_scale = HD ** (-0.5)
    softmax_probs = attend_probs(queries, key_vals)
    weights = softmax_probs.astype(jnp.bfloat16)
    prob_grad = jnp.einsum("glhd,gmhd->ghlm", cotangent, values, preferred_element_type=jnp.float32)
    row_delta = jnp.sum(cotangent.astype(jnp.float32) * attended.astype(jnp.float32), -1)
    row_delta = jnp.transpose(row_delta, (0, 2, 1))[..., None]
    score_grad = (softmax_probs * (prob_grad - row_delta)).astype(jnp.bfloat16)
    grad_query = (
        jnp.einsum("ghlm,gmhd->glhd", score_grad, key_vals, preferred_element_type=jnp.float32)
        * score_scale
    ).astype(jnp.bfloat16)
    grad_keys = (
        jnp.einsum("ghlm,glhd->gmhd", score_grad, queries, preferred_element_type=jnp.float32)
        * score_scale
    ).astype(jnp.bfloat16)
    grad_values = jnp.einsum(
        "ghlm,glhd->gmhd", weights, cotangent, preferred_element_type=jnp.float32
    ).astype(jnp.bfloat16)
    return (grad_query, grad_keys, grad_values)


def body(inputs, norm_gain, qkv_weight, out_weight, out_cotan):
    band_rows = inputs.shape[1]
    columns = inputs.shape[2]
    feature_width = inputs.shape[3]
    seq_count = lax.axis_size("seq")
    all_rows = band_rows * seq_count
    col_share = columns // seq_count
    half_heads = H // 2
    half_width = half_heads * HD
    tokens = band_rows * columns
    flat_input = inputs.reshape(tokens, feature_width).astype(jnp.float32)
    inverse_rms = lax.rsqrt(jnp.mean(flat_input * flat_input, -1, keepdims=True) + 1e-05)
    normed = flat_input * inverse_rms
    hidden = (normed * norm_gain).astype(jnp.bfloat16)
    weight_parts = qkv_weight.reshape(feature_width, 3, H, HD)
    weight_rows = weight_parts[:, :, :half_heads].reshape(feature_width, 3 * half_width)
    weight_cols = weight_parts[:, :, half_heads:].reshape(feature_width, 3 * half_width)
    row_proj = jnp.dot(hidden, weight_rows, preferred_element_type=jnp.float32).astype(jnp.bfloat16)
    row_grid = row_proj.reshape(band_rows, columns, 3, half_heads, HD)
    flat_cotan = out_cotan.reshape(tokens, feature_width)
    grad_att = jnp.dot(flat_cotan, out_weight.T, preferred_element_type=jnp.float32).astype(
        jnp.bfloat16
    )
    att_cot_grid = grad_att.reshape(band_rows, columns, H, HD)
    col_cot = att_cot_grid[:, :, half_heads:].reshape(band_rows, columns, half_width)
    col_group = math.gcd(col_share, max(1, 512 // all_rows))
    col_qkv = (
        jnp.dot(hidden, weight_cols, preferred_element_type=jnp.float32)
        .astype(jnp.bfloat16)
        .reshape(band_rows, columns, 3 * half_width)
    )
    received = lax.all_to_all(col_qkv, "seq", split_axis=1, concat_axis=0, tiled=True)
    col_grid = jnp.swapaxes(received, 0, 1).reshape(col_share, all_rows, 3, half_heads, HD)
    cols_in = (col_grid[:, :, 0], col_grid[:, :, 1], col_grid[:, :, 2])
    col_att = blocked(forward_block, cols_in, col_group)
    sent_att = jnp.swapaxes(col_att, 0, 1).reshape(all_rows, col_share, half_width)
    col_out = lax.all_to_all(sent_att, "seq", split_axis=0, concat_axis=1, tiled=True)
    received_cot = lax.all_to_all(col_cot, "seq", split_axis=1, concat_axis=0, tiled=True)
    cot_grid = jnp.swapaxes(received_cot, 0, 1).reshape(col_share, all_rows, half_heads, HD)
    col_grads = blocked(backward_block, cols_in + (col_att, cot_grid), col_group)
    stacked = jnp.swapaxes(jnp.stack(col_grads, 2), 0, 1).reshape(
        all_rows, col_share, 3 * half_width
    )
    col_dqkv = lax.all_to_all(stacked, "seq", split_axis=0, concat_axis=1, tiled=True)
    row_group = math.gcd(band_rows, max(1, 512 // columns))
    rows_in = (row_grid[:, :, 0], row_grid[:, :, 1], row_grid[:, :, 2])
    row_att = blocked(forward_block, rows_in, row_group)
    row_grads = blocked(
        backward_block, rows_in + (row_att, att_cot_grid[:, :, :half_heads]), row_group
    )
    attended = jnp.concatenate(
        [row_att, col_out.reshape(band_rows, columns, half_heads, HD)], 2
    ).reshape(tokens, feature_width)
    row_dqkv = jnp.stack(row_grads, 2)
    grad_qkv = jnp.concatenate(
        [row_dqkv, col_dqkv.reshape(band_rows, columns, 3, half_heads, HD)], 3
    ).reshape(tokens, 3 * feature_width)
    term_out = jnp.dot(attended.T, flat_cotan, preferred_element_type=jnp.float32)
    term_qkv = jnp.dot(hidden.T, grad_qkv, preferred_element_type=jnp.float32)
    grad_hidden = jnp.dot(grad_qkv, qkv_weight.T, preferred_element_type=jnp.float32)
    term_gain = jnp.sum(grad_hidden * normed, 0)
    grad_normed = grad_hidden * norm_gain
    grad_input = inverse_rms * (
        grad_normed - normed * jnp.mean(grad_normed * normed, -1, keepdims=True)
    )
    input_grad = (
        (flat_cotan.astype(jnp.float32) + grad_input).astype(jnp.bfloat16).reshape(inputs.shape)
    )
    full_qkv, full_out, full_gain = lax.psum((term_qkv, term_out, term_gain), ("seq", "dp"))
    row_share = feature_width // seq_count
    first_row = lax.axis_index("seq") * row_share
    sum_qkv = lax.dynamic_slice_in_dim(full_qkv, first_row, row_share, 0)
    sum_out = lax.dynamic_slice_in_dim(full_out, first_row, row_share, 0)
    sum_gain = lax.dynamic_slice_in_dim(full_gain, first_row, row_share, 0)
    return (input_grad, sum_qkv, sum_out, sum_gain)


def solution(mesh):
    return jax.shard_map(
        body,
        mesh=mesh,
        in_specs=(P("dp", "seq", None, None), P(), P(), P(), P("dp", "seq", None, None)),
        out_specs=(P("dp", "seq", None, None), P("seq", None), P("seq", None), P("seq")),
        check_vma=False,
    )
```

profile of v0, /device:TPU:97, one launch (start us, length us, event | category | flops | bytes accessed | tf_op | source)
XLA Modules:
  0.0 445.4 jit_solution(2909566753671628092)
XLA Ops:
  8.2 1.5 convolution_convert_fusion.4
  11.5 2.2 reduce.5
  14.6 12.3 %all-to-all-start.1 = ((bf16[64,2,1024]{2,1,0:T(2,128)(2,1)}), bf16[64,2,1024]{2,1,0:T(2,128)(2,1)}, u32[]{:S(2)}, u32[]{:S(2)}) async-start(bf16[64,2,1024]{2,1,0:T(2,128)(2,1)} %reshape.245), calls=%async_computation.1 | async-start | bytes 524288 | tf_op jit(solution)/shard_map/all_to_all | solution.py:104
  27.0 1.7 copy.93
  28.8 1.0 fusion.60
  30.5 1.2 copy.168
  31.7 5.4 %reduce.6 = bf16[512,768]{1,0:T(8,128)(2,1)S(1)} reduce(bf16[512,1,768]{2,1,0:T(2,128)(2,1)S(1)} %bitcast.188, bf16[]{:T(256)} %broadcast.106), dimensions={1}, to_apply=%bitcast.186.reduce_sub_computation | reduce | bytes 1572866
  37.1 1.2 reshape.247
  38.3 2.2 all-to-all-done.1
  40.5 10.7 %all-to-all-start = ((bf16[64,2,3072]{2,1,0:T(2,128)(2,1)}), bf16[64,2,3072]{2,1,0:T(2,128)(2,1)}, u32[]{:S(2)}, u32[]{:S(2)}) async-start(bf16[64,2,3072]{2,1,0:T(2,128)(2,1)} %reshape.247), calls=%async_computation | async-start | bytes 1572864 | tf_op jit(solution)/shard_map/all_to_all | solution.py:98
  52.3 3.6 fusion.63
  55.9 2.8 fusion.6
  58.8 2.1 multiply_reduce_fusion
  60.9 2.8 reshape.246
  63.7 1.1 copy.167
  64.7 1.1 copy.151
  65.8 7.4 %all-to-all-done = bf16[64,2,3072]{2,1,0:T(2,128)(2,1)} async-done(((bf16[64,2,3072]{2,1,0:T(2,128)(2,1)}), bf16[64,2,3072]{2,1,0:T(2,128)(2,1)}, u32[]{:S(2)}, u32[]{:S(2)}) %all-to-all-start) | async-done | bytes 786464 | tf_op jit(solution)/shard_map/all_to_all | solution.py:98
  73.2 5.8 %reshape.248 = bf16[512,1,768]{2,1,0:T(2,128)(2,1)} reshape(bf16[64,2,3072]{2,1,0:T(2,128)(2,1)} %all-to-all-done) | data formatting | bytes 1572864
  79.0 2.4 copy.166
  81.4 3.5 reshape.243
  84.9 2.7 fusion.61
  88.1 1.3 fusion.62
  89.4 3.3 fusion.38
  92.7 2.0 copy.141
  94.7 7.6 %all-to-all-start.3 = ((bf16[64,8,256]{2,1,0:T(8,128)(2,1)}), bf16[64,8,256]{2,1,0:T(8,128)(2,1)S(1)}, u32[]{:S(2)}, u32[]{:S(2)}) async-start(bf16[64,8,256]{2,1,0:T(8,128)(2,1)} %copy.141), calls=%async_computation.3 | async-start | bytes 524288 | tf_op jit(solution)/shard_map/all_to_all | solution.py:103
  102.3 2.8 fusion.16
  105.0 3.0 fusion.22
  108.0 1.6 fusion.21
  109.7 1.5 fusion.20
  111.6 2.4 copy.121
  114.0 3.6 reshape.235
  117.6 12.9 %all-to-all-start.2 = ((bf16[64,8,768]{2,1,0:T(8,128)(2,1)}), bf16[64,8,768]{2,1,0:T(8,128)(2,1)}, u32[]{:S(2)}, u32[]{:S(2)}) async-start(bf16[64,8,768]{2,1,0:T(8,128)(2,1)} %reshape.235), calls=%async_computation.2 | async-start | bytes 1572864 | tf_op jit(solution)/shard_map/all_to_all | solution.py:110
  130.6 1.8 fusion.28
  132.4 2.9 multiply_convert_fusion
  135.4 1.5 fusion.25
  136.8 1.2 fusion.26
  138.7 1.4 fusion.41
  140.1 13.3 %all-to-all-done.2 = bf16[64,8,768]{2,1,0:T(8,128)(2,1)} async-done(((bf16[64,8,768]{2,1,0:T(8,128)(2,1)}), bf16[64,8,768]{2,1,0:T(8,128)(2,1)}, u32[]{:S(2)}, u32[]{:S(2)}) %all-to-all-start.2) | async-done | bytes 786464 | tf_op jit(solution)/shard_map/all_to_all | solution.py:110
  153.4 2.8 reshape.236
  156.1 2.3 copy.122
  158.4 1.4 pad_maximum_fusion
  159.9 2.9 fusion.54
  162.8 3.6 fusion.34
  166.4 78.7 %psum.23 = f32[512]{0:T(512)S(1)} all-reduce(f32[512]{0:T(512)S(1)} %get-tuple-element.60), channel_id=1, replica_groups=mesh['seq'=64,'dp'=4] {'seq','dp'}, use_global_device_ids=true, to_apply=%region_11.12 | all-reduce | flops 512 | bytes 4096 | tf_op jit(solution)/shard_map/psum | solution.py:135
  245.7 2.4 fusion.40
  248.0 187.8 %all-reduce.3.cloned.1.call-done = (f32[512,1536]{1,0:T(8,128)}, f32[512,512]{1,0:T(8,128)}) async-done(((f32[512,1536]{1,0:T(8,128)}, f32[512,512]{1,0:T(8,128)}), (f32[512,1536]{1,0:T(8,128)}, f32[512,512]{1,0:T(8,128)})) %all-reduce.3.cloned.1.call-update) | async-done | bytes 4194320 | tf_op jit(solution)/shard_map/psum | solution.py:135
  435.8 1.4 constant_dynamic-slice_fusion.1
  437.2 1.3 constant_dynamic-slice_fusion
  (55 shorter events, 7.6 us)
Async XLA Ops:
  7.2 1.0 copy-start
  7.2 19.7 %copy-start.1 = (bf16[1,1,512,512]{3,2,1,0:T(8,128)(2,1)S(1)}, bf16[1,1,512,512]{3,2,1,0:T(8,128)(2,1)}, u32[]{:S(2)}) copy-start(bf16[1,1,512,512]{3,2,1,0:T(8,128)(2,1)} %param.5) | copy-start | bytes 1572868
  9.7 0.8 copy-start.3
  14.6 26.0 %all-to-all-start.1 = ((bf16[64,2,1024]{2,1,0:T(2,128)(2,1)}), bf16[64,2,1024]{2,1,0:T(2,128)(2,1)}, u32[]{:S(2)}, u32[]{:S(2)}) async-start(bf16[64,2,1024]{2,1,0:T(2,128)(2,1)} %reshape.245), calls=%async_computation.1 | async-start | bytes 524288 | tf_op jit(solution)/shard_map/all_to_all | solution.py:104
  28.8 1.0 copy-start.16
  37.1 14.1 %copy-start.14 = (bf16[512,3,4,64]{0,3,2,1:T(8,128)(2,1)S(1)}, bf16[512,3,4,64]{0,3,2,1:T(8,128)(2,1)}, u32[]{:S(2)}) copy-start(bf16[512,3,4,64]{0,3,2,1:T(8,128)(2,1)} %get-tuple-element.69) | copy-start | bytes 2359300
  40.5 32.7 %all-to-all-start = ((bf16[64,2,3072]{2,1,0:T(2,128)(2,1)}), bf16[64,2,3072]{2,1,0:T(2,128)(2,1)}, u32[]{:S(2)}, u32[]{:S(2)}) async-start(bf16[64,2,3072]{2,1,0:T(2,128)(2,1)} %reshape.247), calls=%async_computation | async-start | bytes 1572864 | tf_op jit(solution)/shard_map/all_to_all | solution.py:98
  52.2 3.7 copy-start.6
  55.9 2.8 copy-start.4
  87.6 1.8 copy-start.8
  87.6 1.8 copy-start.9
  88.1 1.3 copy-start.12
  94.7 22.9 %all-to-all-start.3 = ((bf16[64,8,256]{2,1,0:T(8,128)(2,1)}), bf16[64,8,256]{2,1,0:T(8,128)(2,1)S(1)}, u32[]{:S(2)}, u32[]{:S(2)}) async-start(bf16[64,8,256]{2,1,0:T(8,128)(2,1)} %copy.141), calls=%async_computation.3 | async-start | bytes 524288 | tf_op jit(solution)/shard_map/all_to_all | solution.py:103
  108.0 3.2 copy-start.15
  117.6 12.9 %copy-start.10 = (bf16[64,8,256]{2,1,0:T(8,128)(2,1)}, bf16[64,8,256]{2,1,0:T(8,128)(2,1)S(1)}, u32[]{:S(2)}) copy-start(bf16[64,8,256]{2,1,0:T(8,128)(2,1)S(1)} %all-to-all-done.3) | copy-start | bytes 786436
  117.6 35.8 %all-to-all-start.2 = ((bf16[64,8,768]{2,1,0:T(8,128)(2,1)}), bf16[64,8,768]{2,1,0:T(8,128)(2,1)}, u32[]{:S(2)}, u32[]{:S(2)}) async-start(bf16[64,8,768]{2,1,0:T(8,128)(2,1)} %reshape.235), calls=%async_computation.2 | async-start | bytes 1572864 | tf_op jit(solution)/shard_map/all_to_all | solution.py:110
  130.5 305.3 %all-reduce.3.cloned.1.call-start = ((), (), s32[]{:S(2)}) async-start(), calls=%async_computation.4 | async-start | bytes 8388608 | tf_op jit(solution)/shard_map/psum | solution.py:135
  130.6 1.8 copy-start.5
  130.6 1.8 copy-start.7
  135.4 2.7 copy-start.11
  136.8 1.8 copy-start.13
  136.8 1.8 copy-start.2
Sparse Core Ops, SparseCore 0:
  162.9 272.8 all-reduce.2
where the time goes:
time: 447 us; the launch traced here: 445 us
  waiting for transfers between devices  211 us (47%)
  blocking collectives  78.7 us (18%)
  local copies, waits for them, and re-layouts  45.3 us (10%)
  starting transfers between devices  43.5 us (10%)
  matrix products  36.5 us (8%)
  other arithmetic  16.3 us (4%)
  between operations  14.4 us (3%)
    psum x1, waiting for transfers between devices, body(): lax.psum((term_qkv, term_out, term_gain), ('seq', 'dp'))  188 us
    psum x1, blocking collectives, body(): lax.psum((term_qkv, term_out, term_gain), ('seq', 'dp'))  78.7 us
    unnamed x42, local copies, waits for them, and re-layouts  18.2 us
    all_to_all x1, waiting for transfers between devices, body(): lax.all_to_all(stacked, 'seq', split_axis=0, concat_axis=1, tiled=True)  13.3 us
    all_to_all x1, starting transfers between devices, body(): lax.all_to_all(stacked, 'seq', split_axis=0, concat_axis=1, tiled=True)  12.9 us
    all_to_all x1, starting transfers between devices, body(): lax.all_to_all(col_cot, 'seq', split_axis=1, concat_axis=0, tiled=True)  12.3 us
    all_to_all x1, starting transfers between devices, body(): lax.all_to_all(col_qkv, 'seq', split_axis=1, concat_axis=0, tiled=True)  10.7 us
  transfers between devices with their start and end apart: 5, of which 4 were waited for; matrix products, arithmetic and copies ran while one was open for 13% of the time, Pallas kernels for 0%

commit v1 on v0

--- a/solution.py
+++ b/solution.py
@@ -132,7 +132,7 @@
     input_grad = (
         (flat_cotan.astype(jnp.float32) + grad_input).astype(jnp.bfloat16).reshape(inputs.shape)
     )
-    full_qkv, full_out, full_gain = lax.psum((term_qkv, term_out, term_gain), ("seq", "dp"))
+    full_qkv, full_out, full_gain = lax.psum(lax.psum((term_qkv, term_out, term_gain), "seq"), "dp")
     row_share = feature_width // seq_count
     first_row = lax.axis_index("seq") * row_share
     sum_qkv = lax.dynamic_slice_in_dim(full_qkv, first_row, row_share, 0)

time: 447 us -> 1240 us (2.77); the launches traced: 445 us -> 1220 us
  waiting for transfers between devices: 211 us -> 820 us
  blocking collectives: 78.7 us -> 245 us
    psum x1 -> x2, waiting for transfers between devices: 188 us -> 797 us  [the longest x1 797 us: body(): lax.psum((term_qkv, term_out, term_gain), 'seq')]
    psum x1 -> x2, blocking collectives: 78.7 us -> 245 us  [the longest x1 209 us: body(): lax.psum((term_qkv, term_out, term_gain), 'seq')]
  transfers between devices with their start and end apart: 5 -> 6, of which waited for: 4 -> 4; matrix products, arithmetic and copies ran while one was open for 13% -> 5% of each run, Pallas kernels for 0% -> 0%
where the time goes in v1:
time: 1240 us; the launch traced here: 1220 us
  waiting for transfers between devices  820 us (66%)
  blocking collectives  245 us (20%)
  local copies, waits for them, and re-layouts  45.3 us (4%)
  starting transfers between devices  43.6 us (4%)
  matrix products  36.5 us (3%)
  other arithmetic  16.3 us (1%)
  between operations  14.4 us (1%)
    psum x1, waiting for transfers between devices, body(): lax.psum((term_qkv, term_out, term_gain), 'seq')  797 us
    psum x1, blocking collectives, body(): lax.psum((term_qkv, term_out, term_gain), 'seq')  209 us
    psum x1, blocking collectives, body(): lax.psum(lax.psum((term_qkv, term_out, term_gain), 'seq'), 'dp')  36.5 us
  transfers between devices with their start and end apart: 6, of which 4 were waited for; matrix products, arithmetic and copies ran while one was open for 5% of the time, Pallas kernels for 0%

profile of v1, /device:TPU:97, one launch (start us, length us, event | category | flops | bytes accessed | tf_op | source)
XLA Modules:
  0.0 1221.5 jit_solution(8506878034471749433)
XLA Ops:
  8.2 1.5 convolution_convert_fusion.4
  11.5 2.2 reduce.5
  14.6 12.3 %all-to-all-start.1 = ((bf16[64,2,1024]{2,1,0:T(2,128)(2,1)}), bf16[64,2,1024]{2,1,0:T(2,128)(2,1)}, u32[]{:S(2)}, u32[]{:S(2)}) async-start(bf16[64,2,1024]{2,1,0:T(2,128)(2,1)} %reshape.245), calls=%async_computation.1 | async-start | bytes 524288 | tf_op jit(solution)/shard_map/all_to_all | solution.py:104
  27.0 1.7 copy.93
  30.5 1.2 copy.168
  31.7 5.4 reduce.6
  37.1 1.2 reshape.247
  38.3 2.2 all-to-all-done.1
  40.5 10.7 all-to-all-start
  52.3 3.6 fusion.63
  55.9 2.8 fusion.6
  58.8 2.1 multiply_reduce_fusion
  60.9 2.8 reshape.246
  63.7 1.1 copy.167
  64.7 1.1 copy.151
  65.8 7.4 all-to-all-done
  73.2 5.8 reshape.248
  79.0 2.4 copy.166
  81.4 3.5 reshape.243
  84.9 2.7 fusion.61
  88.1 1.3 fusion.62
  89.4 3.3 fusion.38
  92.7 2.0 copy.141
  94.7 7.6 all-to-all-start.3
  102.3 2.8 fusion.16
  105.0 3.0 fusion.22
  108.0 1.6 fusion.21
  109.6 1.5 fusion.20
  111.6 2.4 copy.121
  114.0 3.6 reshape.235
  117.6 12.9 %all-to-all-start.2 = ((bf16[64,8,768]{2,1,0:T(8,128)(2,1)}), bf16[64,8,768]{2,1,0:T(8,128)(2,1)}, u32[]{:S(2)}, u32[]{:S(2)}) async-start(bf16[64,8,768]{2,1,0:T(8,128)(2,1)} %reshape.235), calls=%async_computation.2 | async-start | bytes 1572864 | tf_op jit(solution)/shard_map/all_to_all | solution.py:110
  130.6 1.8 fusion.28
  132.4 2.9 multiply_convert_fusion
  135.3 1.5 fusion.25
  136.8 1.2 fusion.26
  138.6 1.4 fusion.41
  140.1 13.3 %all-to-all-done.2 = bf16[64,8,768]{2,1,0:T(8,128)(2,1)} async-done(((bf16[64,8,768]{2,1,0:T(8,128)(2,1)}), bf16[64,8,768]{2,1,0:T(8,128)(2,1)}, u32[]{:S(2)}, u32[]{:S(2)}) %all-to-all-start.2) | async-done | bytes 786464 | tf_op jit(solution)/shard_map/all_to_all | solution.py:110
  153.3 2.8 reshape.236
  156.1 2.3 copy.122
  158.4 1.4 pad_maximum_fusion
  159.8 2.9 fusion.54
  162.8 797.1 %all-reduce.5.cloned.1.call-done = (f32[512,1536]{1,0:T(8,128)}, f32[512,512]{1,0:T(8,128)}) async-done(((f32[512,1536]{1,0:T(8,128)}, f32[512,512]{1,0:T(8,128)}), (f32[512,1536]{1,0:T(8,128)}, f32[512,512]{1,0:T(8,128)})) %all-reduce.5.cloned.1.call-update) | async-done | bytes 4194320 | tf_op jit(solution)/shard_map/psum | solution.py:135
  960.0 3.6 fusion.34
  963.6 208.9 %psum.46 = f32[512]{0:T(512)S(1)} all-reduce(f32[512]{0:T(512)S(1)} %get-tuple-element.60), channel_id=1, replica_groups=mesh['seq'=64,'dp'=4] {'seq'}, use_global_device_ids=true, to_apply=%region_13.14 | all-reduce | flops 512 | bytes 4096 | tf_op jit(solution)/shard_map/psum | solution.py:135
  1172.5 36.5 %psum.47 = f32[512]{0:T(512)S(1)} all-reduce(f32[512]{0:T(512)S(1)} %psum.46), channel_id=1, replica_groups=mesh['seq'=64,'dp'=4] {'dp'}, use_global_device_ids=true, to_apply=%region_14.15 | all-reduce | flops 512 | bytes 4096 | tf_op jit(solution)/shard_map/psum | solution.py:135
  1209.5 2.4 fusion.40
  1211.9 1.4 constant_dynamic-slice_fusion.1
  1213.3 1.3 constant_dynamic-slice_fusion
  (59 shorter events, 8.7 us)
Async XLA Ops:
  7.2 1.0 copy-start
  7.2 19.7 %copy-start.1 = (bf16[1,1,512,512]{3,2,1,0:T(8,128)(2,1)S(1)}, bf16[1,1,512,512]{3,2,1,0:T(8,128)(2,1)}, u32[]{:S(2)}) copy-start(bf16[1,1,512,512]{3,2,1,0:T(8,128)(2,1)} %param.5) | copy-start | bytes 1572868
  9.7 0.8 copy-start.3
  14.6 26.0 %all-to-all-start.1 = ((bf16[64,2,1024]{2,1,0:T(2,128)(2,1)}), bf16[64,2,1024]{2,1,0:T(2,128)(2,1)}, u32[]{:S(2)}, u32[]{:S(2)}) async-start(bf16[64,2,1024]{2,1,0:T(2,128)(2,1)} %reshape.245), calls=%async_computation.1 | async-start | bytes 524288 | tf_op jit(solution)/shard_map/all_to_all | solution.py:104
  28.8 1.0 copy-start.16
  37.1 14.1 %copy-start.14 = (bf16[512,3,4,64]{0,3,2,1:T(8,128)(2,1)S(1)}, bf16[512,3,4,64]{0,3,2,1:T(8,128)(2,1)}, u32[]{:S(2)}) copy-start(bf16[512,3,4,64]{0,3,2,1:T(8,128)(2,1)} %get-tuple-element.76) | copy-start | bytes 2359300
  40.5 32.7 %all-to-all-start = ((bf16[64,2,3072]{2,1,0:T(2,128)(2,1)}), bf16[64,2,3072]{2,1,0:T(2,128)(2,1)}, u32[]{:S(2)}, u32[]{:S(2)}) async-start(bf16[64,2,3072]{2,1,0:T(2,128)(2,1)} %reshape.247), calls=%async_computation | async-start | bytes 1572864 | tf_op jit(solution)/shard_map/all_to_all | solution.py:98
  52.2 3.7 copy-start.6
  55.9 2.8 copy-start.4
  87.6 1.8 copy-start.8
  87.6 1.8 copy-start.9
  88.1 1.3 copy-start.12
  94.7 22.8 %all-to-all-start.3 = ((bf16[64,8,256]{2,1,0:T(8,128)(2,1)}), bf16[64,8,256]{2,1,0:T(8,128)(2,1)S(1)}, u32[]{:S(2)}, u32[]{:S(2)}) async-start(bf16[64,8,256]{2,1,0:T(8,128)(2,1)} %copy.141), calls=%async_computation.3 | async-start | bytes 524288 | tf_op jit(solution)/shard_map/all_to_all | solution.py:103
  108.0 3.2 copy-start.15
  117.6 12.9 %copy-start.10 = (bf16[64,8,256]{2,1,0:T(8,128)(2,1)}, bf16[64,8,256]{2,1,0:T(8,128)(2,1)S(1)}, u32[]{:S(2)}) copy-start(bf16[64,8,256]{2,1,0:T(8,128)(2,1)S(1)} %all-to-all-done.3) | copy-start | bytes 786436
  117.6 35.8 %all-to-all-start.2 = ((bf16[64,8,768]{2,1,0:T(8,128)(2,1)}), bf16[64,8,768]{2,1,0:T(8,128)(2,1)}, u32[]{:S(2)}, u32[]{:S(2)}) async-start(bf16[64,8,768]{2,1,0:T(8,128)(2,1)} %reshape.235), calls=%async_computation.2 | async-start | bytes 1572864 | tf_op jit(solution)/shard_map/all_to_all | solution.py:110
  130.5 829.4 %all-reduce.5.cloned.1.call-start = ((), (), s32[]{:S(2)}) async-start(), calls=%async_computation.4 | async-start | bytes 8388608 | tf_op jit(solution)/shard_map/psum | solution.py:135
  130.5 1.8 copy-start.5
  130.6 1.8 copy-start.7
  135.3 2.7 copy-start.11
  136.8 1.8 copy-start.13
  136.8 1.8 copy-start.2
  162.8 1049.1 %all-reduce.7.cloned.1.call-start = ((), (), s32[]{:S(2)}) async-start(), calls=%async_computation.5 | async-start | bytes 8388608 | tf_op jit(solution)/shard_map/psum | solution.py:135
Sparse Core Ops, SparseCore 0:
  162.9 796.9 all-reduce.4
  962.7 167.4 all-reduce.6
